TPU v7x, 32 devices: a whole 2x2x4 slice. The times are simulated.
32 devices in a mesh: dp: 2 (over x), seq: 16 (over z, y, core).
Axes of the slice: x: 2, y: 2, z: 4, core: 2. Of those that a mesh axis runs over, the one named last changes fastest.
Arguments:
- queries: bfloat16 [4096, 1024], P(('dp', 'seq')), parts along dimension 0, may hold values from -6 to 6
- keys: bfloat16 [4096, 1024], P(('dp', 'seq')), parts along dimension 0, may hold values from -6 to 6
- values: bfloat16 [4096, 1024], P(('dp', 'seq')), parts along dimension 0, may hold values from -36 to 36
- feat_weight: bfloat16 [16, 64, 256], replicated, may hold values from -0.75 to 0.75
- norm_gain: bfloat16 [1024], replicated, may hold values from 0.25 to 1.75
- counts: int32 [32, 16], P('dp'), parts along dimension 0, may hold values from 4 to 12, as said below
- offsets: int32 [32, 16], P('dp'), parts along dimension 0, may hold values from 0 to 127, as said below
Outputs:
- mixed: bfloat16 [4096, 1024], P(('dp', 'seq')), parts along dimension 0
There are 2 independent parts, one for each index of `dp`. A program takes and returns all parts, laid end to end along the dimension named above; an argument that names none is the same for every part. Nothing has to cross between parts.
Inputs may be any that keep to these rules, and one draw needn't show every extreme that they name: Each row and each column of counts sums to 128; every loader sends 12 rows to exactly one device. For each device d the ranges from offsets[j, d] to offsets[j, d] + counts[j, d] - 1 over all loaders j tile 0 to 127.
All inputs are finite; a program needn't handle non-finite values.
Results may differ from a plain program's by a relative error of at most 0.0023.
Values may be sent and summed in bfloat16 or wider, within the bound.
A program may use at most 192 MiB of HBM per device.

v0:
```python
import functools

import jax
import jax.numpy as jnp
from jax import lax
from jax.experimental import pallas as pl
from jax.experimental.pallas import tpu as pltpu
from jax.sharding import PartitionSpec as P

MESH = pl.DeviceIdType.MESH
F32 = jnp.float32
BF16 = jnp.bfloat16
GROUPS = 4


def kernel(
    n,
    heads,
    q_ref,
    k_ref,
    v_ref,
    w_ref,
    gain_ref,
    counts_ref,
    offsets_ref,
    out_ref,
    q_buf,
    k_buf,
    v_buf,
    w_buf,
    gain_buf,
    counts_buf,
    offsets_buf,
    load_sem,
    send,
    recv,
    phi_q,
    phi_kt,
    val,
    posr,
    post,
    posc,
    slot_row,
    slot_col,
    acc,
    wq,
    wkt,
    out_send,
    out_recv,
    send_sem,
    recv_sem,
    back_send_sem,
    back_recv_sem,
):
    rows = q_ref.shape[0]
    half = rows // 2
    width = q_ref.shape[1] // heads
    feat = w_ref.shape[2]
    group = n // heads
    part_rows = rows // group
    part_half = part_rows // 2
    total = n * rows
    queries = n * part_rows
    me = lax.axis_index("seq")
    head = me // group
    part = me % group

    half_ring = n // 2
    own = me // half_ring * half_ring
    other = lax.rem(own + half_ring, n)

    def target(step):
        return jnp.where(step < half_ring, own, other) + lax.rem(me + step, half_ring)

    def source(step):
        return jnp.where(step < half_ring, own, other) + lax.rem(me + n - step, half_ring)

    loads = [
        pltpu.make_async_copy(src, dst, load_sem.at[i])
        for i, (src, dst) in enumerate(
            (
                (q_ref, q_buf),
                (k_ref, k_buf),
                (v_ref, v_buf),
                (counts_ref, counts_buf),
                (offsets_ref, offsets_buf),
                (w_ref.at[head], w_buf),
                (gain_ref, gain_buf),
            )
        )
    ]
    for load in loads:
        load.start()

    barrier = pltpu.get_barrier_semaphore()

    def greet(step, carry):
        peer = lax.rem(me + step, n)
        pl.semaphore_signal(barrier, inc=1, device_id={"seq": peer}, device_id_type=MESH)
        return carry

    lax.fori_loop(1, n, greet, 0)

    for load in loads[:3]:
        load.wait()

    for pair in range(heads // 2):
        lanes = slice(2 * width * pair, 2 * width * (pair + 1))
        q = q_buf[:, lanes]
        k = k_buf[:, lanes]
        v = v_buf[:, lanes]
        send[2 * pair, 0:rows, :] = jnp.concatenate([q[:, :width], k[:, :width]], axis=1)
        send[2 * pair + 1, 0:rows, :] = jnp.concatenate([q[:, width:], k[:, width:]], axis=1)
        send[2 * pair, rows:, :] = jnp.concatenate([v[:half, :width], v[half:, :width]], axis=1)
        send[2 * pair + 1, rows:, :] = jnp.concatenate([v[:half, width:], v[half:, width:]], axis=1)

    pl.semaphore_wait(barrier, n - 1)

    def forward(peer):
        return pltpu.make_async_remote_copy(
            src_ref=send.at[peer // group],
            dst_ref=recv.at[me],
            send_sem=send_sem.at[peer],
            recv_sem=recv_sem.at[me],
            device_id={"seq": peer},
            device_id_type=MESH,
        )

    def send_one(step, carry):
        forward(target(step)).start()
        return carry

    lax.fori_loop(1, n, send_one, 0)
    recv[me] = send[head]

    for load in loads[3:]:
        load.wait()

    lane = lax.broadcasted_iota(jnp.int32, (n, rows), 1)
    start = jnp.zeros((n, 1), jnp.int32)
    position = lane
    for d in range(n):
        count = counts_buf[:, d : d + 1]
        inside = (lane >= start) & (lane < start + count)
        position = position + jnp.where(inside, d * rows + offsets_buf[:, d : d + 1] - start, 0)
        start = start + count
    position = position.astype(F32)
    posr[...] = position
    if n < rows:
        position = jnp.concatenate([position, jnp.zeros((rows - n, rows), F32)], axis=0)
    post[...] = position.T
    mine = post[pl.ds(pl.multiple_of(part * part_rows, part_rows), part_rows), :]
    for j in range(n):
        posc[j * part_rows : (j + 1) * part_rows, :] = jnp.broadcast_to(
            mine[:, j : j + 1], (part_rows, 128)
        )

    w = w_buf[...]
    blank = jnp.zeros_like(w)
    wq[...] = jnp.concatenate([w, blank], axis=0)
    wkt[...] = jnp.concatenate([blank, w], axis=0).astype(F32).T.astype(BF16)
    gain = jnp.zeros((1, width), F32)
    for h in range(heads):
        gain = gain + jnp.where(head == h, gain_buf[:, h * width : (h + 1) * width].astype(F32), 0.0)

    def feature(z):
        return jnp.where(z > 0.0, z + 1.0, jnp.exp(jnp.minimum(z, 0.0))).astype(BF16)

    def take_block(step):
        src = source(step)
        x = recv[src, 0:rows, :]
        keys = lax.dot_general(wkt[...], x, (((1,), (1,)), ((), ())), preferred_element_type=F32)
        phi_kt[:, step * rows : (step + 1) * rows] = feature(keys)
        mine_of = pl.multiple_of(part * part_rows, part_rows)
        proj = jnp.dot(
            recv[src, pl.ds(mine_of, part_rows), :], wq[...], preferred_element_type=F32
        )
        slots = slice(step * part_rows, (step + 1) * part_rows)
        phi_q[slots, :] = feature(proj)
        block = recv[src, rows:, :]
        val[step * rows : step * rows + half, :] = block[:, :width]
        val[step * rows + half : (step + 1) * rows, :] = block[:, width:]
        slot_row[step : step + 1, :] = posr[pl.ds(src, 1), :]
        slot_col[slots, :] = posc[
            pl.ds(pl.multiple_of(src * part_rows, part_rows), part_rows), :
        ]

    def arrive(step):
        src = source(step)
        pltpu.make_async_remote_copy(
            src_ref=send.at[0],
            dst_ref=recv.at[src],
            send_sem=send_sem.at[src],
            recv_sem=recv_sem.at[src],
            device_id={"seq": src},
            device_id_type=MESH,
        ).wait_recv()

    groups = min(GROUPS, n)
    per = n // groups
    tile_r = per * part_rows
    tile_s = per * rows

    def tile(rb, sb):
        r0 = pl.multiple_of(rb * tile_r, tile_r)
        s0 = pl.multiple_of(sb * tile_s, tile_s)
        scores = jnp.dot(
            phi_q[pl.ds(r0, tile_r), :], phi_kt[:, pl.ds(s0, tile_s)], preferred_element_type=F32
        )
        later = jnp.concatenate([slot_col[pl.ds(r0, tile_r), :]] * per, axis=1)
        earlier = jnp.concatenate([slot_row[pl.ds(sb * per + i, 1), :] for i in range(per)], axis=1)
        scores = jnp.where(earlier <= later, scores, 0.0)
        high = scores.astype(BF16)
        low = (scores - high.astype(F32)).astype(BF16)
        vals = val[pl.ds(s0, tile_s), :]
        return jnp.dot(high, vals, preferred_element_type=F32) + jnp.dot(
            low, vals, preferred_element_type=F32
        )

    def back(step):
        loader = source(step)
        return pltpu.make_async_remote_copy(
            src_ref=out_send.at[step],
            dst_ref=out_recv.at[me],
            send_sem=back_send_sem.at[loader],
            recv_sem=back_recv_sem.at[me],
            device_id={"seq": loader},
            device_id_type=MESH,
        )

    def finish(rb, attended):
        centre = jnp.mean(attended, axis=1, keepdims=True)
        centred = attended - centre
        spread = jnp.mean(centred * centred, axis=1, keepdims=True)
        normed = (centred * lax.rsqrt(spread + 1e-05) * gain).astype(BF16)
        for i in range(per):
            y = normed[i * part_rows : (i + 1) * part_rows]
            out_send[rb * per + i] = jnp.concatenate([y[:part_half], y[part_half:]], axis=1)
        for i in range(per):
            if rb * per + i > 0:
                back(rb * per + i).start()

    def rows_of(rb):
        return pl.ds(pl.multiple_of(rb * tile_r, tile_r), tile_r)

    for gi in range(groups):
        for step in range(gi * per, (gi + 1) * per):
            if step > 0:
                arrive(step)
            take_block(step)
        last = gi == groups - 1
        fresh = tile(gi, gi)
        if not last:

            def both(i, fresh):
                acc[rows_of(i), :] = acc[rows_of(i), :] + tile(i, gi)
                return fresh + tile(gi, i)

            acc[rows_of(gi), :] = lax.fori_loop(0, gi, both, fresh)
        else:
            finish(gi, lax.fori_loop(0, gi, lambda i, fresh: fresh + tile(gi, i), fresh))
            for i in reversed(range(gi)):
                finish(i, acc[rows_of(i), :] + tile(i, gi))
    out_recv[me] = out_send[0]

    def collect(step, carry):
        src = source(step)
        pltpu.make_async_remote_copy(
            src_ref=out_send.at[step],
            dst_ref=out_recv.at[src],
            send_sem=back_send_sem.at[src],
            recv_sem=back_recv_sem.at[src],
            device_id={"seq": src},
            device_id_type=MESH,
        ).wait_recv()
        return carry

    lax.fori_loop(1, n, collect, 0)

    for piece in range(group):
        first = slice(piece * part_rows, piece * part_rows + part_half)
        second = slice(piece * part_rows + part_half, (piece + 1) * part_rows)
        for pair in range(heads // 2):
            lanes = slice(2 * width * pair, 2 * width * (pair + 1))
            a = out_recv[2 * pair * group + piece]
            b = out_recv[(2 * pair + 1) * group + piece]
            out_ref[first, lanes] = jnp.concatenate([a[:, :width], b[:, :width]], axis=1)
            out_ref[second, lanes] = jnp.concatenate([a[:, width:], b[:, width:]], axis=1)

    def drain(step, carry):
        peer = target(step)
        forward(peer).wait_send()
        back(step).wait_send()
        return carry

    lax.fori_loop(1, n, drain, 0)


def per_device(n, queries, keys, values, feat_weight, norm_gain, counts, offsets):
    rows = queries.shape[0]
    heads, width, feat = feat_weight.shape
    group = n // heads
    part_rows = rows // group
    total = n * rows
    lanes = 2 * width
    return pl.pallas_call(
        functools.partial(kernel, n, heads),
        out_shape=jax.ShapeDtypeStruct(queries.shape, BF16),
        in_specs=[pl.BlockSpec(memory_space=pltpu.HBM)] * 7,
        out_specs=pl.BlockSpec(memory_space=pltpu.VMEM),
        scratch_shapes=[
            pltpu.VMEM(queries.shape, BF16),
            pltpu.VMEM(keys.shape, BF16),
            pltpu.VMEM(values.shape, BF16),
            pltpu.VMEM((width, feat), BF16),
            pltpu.VMEM((1, norm_gain.shape[0]), BF16),
            pltpu.VMEM(counts.shape, jnp.int32),
            pltpu.VMEM(offsets.shape, jnp.int32),
            pltpu.SemaphoreType.DMA((7,)),
            pltpu.VMEM((heads, rows + rows // 2, lanes), BF16),
            pltpu.VMEM((n, rows + rows // 2, lanes), BF16),
            pltpu.VMEM((n * part_rows, feat), BF16),
            pltpu.VMEM((feat, total), BF16),
            pltpu.VMEM((total, width), BF16),
            pltpu.VMEM((n, rows), F32),
            pltpu.VMEM((rows, max(n, rows)), F32),
            pltpu.VMEM((n * part_rows, 128), F32),
            pltpu.VMEM((n, rows), F32),
            pltpu.VMEM((n * part_rows, 128), F32),
            pltpu.VMEM((n * part_rows, width), F32),
            pltpu.VMEM((lanes, feat), BF16),
            pltpu.VMEM((feat, lanes), BF16),
            pltpu.VMEM((n, part_rows // 2, lanes), BF16),
            pltpu.VMEM((n, part_rows // 2, lanes), BF16),
            pltpu.SemaphoreType.DMA((n,)),
            pltpu.SemaphoreType.DMA((n,)),
            pltpu.SemaphoreType.DMA((n,)),
            pltpu.SemaphoreType.DMA((n,)),
        ],
        compiler_params=pltpu.CompilerParams(
            collective_id=0, has_side_effects=True, vmem_limit_bytes=67043328
        ),
    )(queries, keys, values, feat_weight, norm_gain.reshape(1, -1), counts, offsets)


def solution(mesh):
    in_specs = (
        P(("dp", "seq"), None),
        P(("dp", "seq"), None),
        P(("dp", "seq"), None),
        P(),
        P(),
        P("dp", None),
        P("dp", None),
    )
    return jax.shard_map(
        functools.partial(per_device, mesh.shape["seq"]),
        mesh=mesh,
        in_specs=in_specs,
        out_specs=P(("dp", "seq"), None),
        check_vma=False,
    )
```

profile of v0, /device:TPU:0, one launch (start us, length us, event | category | flops | bytes accessed | tf_op | source)
XLA Modules:
  0.0 39.4 jit_solution(16823842896328260929)
XLA Ops:
  0.0 1.3 %reshape.3.gain_ref = bf16[1,1024]{1,0:T(2,128)(2,1)} reshape(bf16[1024]{0:T(1024)(128)(2,1)} %param.11) | data formatting | bytes 4096 | tf_op jit(solution)/shard_map/reshape | solution.py:343
  1.3 36.5 %shard_map.73 = bf16[128,1024]{1,0:T(8,128)(2,1)} custom-call(bf16[128,1024]{1,0:T(8,128)(2,1)} %q_ref.1, bf16[128,1024]{1,0:T(8,128)(2,1)} %k_ref.1, bf16[128,1024]{1,0:T(8,128)(2,1)} %v_ref.1, bf16[16,64,256]{2,1,0:T(8,128)(2,1)} %w_ref.1, bf16[1,1024]{1,0:T(2,128)(2,1)} %reshape.3.gain_ref, s32[16,16]{1,0:T(8,128)} %counts_ref.1, s32[16,16]{1,0:T(8,128)} %offsets_ref.1), custom_call_target="tpu_custom_call" | custom-call | tf_op jit(solution)/shard_map/pallas_call | solution.py:306
  37.7 1.7 %copy.9 = bf16[128,1024]{1,0:T(8,128)(2,1)} copy(bf16[128,1024]{1,0:T(8,128)(2,1)} %shard_map.73) | data formatting | bytes 524288
where the time goes:
time: 39.6 us; the launch traced here: 39.4 us
  Pallas kernels  36.5 us (92%)
  local copies, waits for them, and re-layouts  2.95 us (7%)
    pallas_call x1, Pallas kernels, per_device(): pl.pallas_call(functools.partial(kernel, n, heads), out_shape=jax.ShapeDt...  36.5 us
    unnamed x1, local copies, waits for them, and re-layouts  1.67 us
    reshape x1, local copies, waits for them, and re-layouts, per_device(): norm_gain.reshape(1, -1)  1.28 us

commit v1 on v0

v1 whole, which is shorter than its diff:
```python
import functools

import jax
import jax.numpy as jnp
from jax import lax
from jax.experimental import pallas as pl
from jax.experimental.pallas import tpu as pltpu
from jax.sharding import PartitionSpec as P

MESH = pl.DeviceIdType.MESH
F32 = jnp.float32
BF16 = jnp.bfloat16
GROUPS = 4


def kernel(
    n,
    heads,
    q_ref,
    k_ref,
    v_ref,
    w_ref,
    gain_ref,
    counts_ref,
    offsets_ref,
    out_ref,
    q_buf,
    k_buf,
    v_buf,
    w_buf,
    gain_buf,
    counts_buf,
    offsets_buf,
    load_sem,
    kv_send,
    kv_recv,
    q_send,
    q_recv,
    phi_kt,
    phi_q,
    posr,
    post,
    posc,
    acc,
    wqa,
    wqb,
    wkt,
    out_send,
    out_recv,
    kv_send_sem,
    kv_recv_sem,
    q_send_sem,
    q_recv_sem,
    back_send_sem,
    back_recv_sem,
):
    rows = q_ref.shape[0]
    width = q_ref.shape[1] // heads
    group = n // heads
    part_rows = rows // group
    part_half = part_rows // 2
    me = lax.axis_index("seq")
    head = me // group
    part = me % group
    near = n // 2

    def partner(step):
        return jnp.bitwise_xor(me, step)

    loads = [
        pltpu.make_async_copy(src, dst, load_sem.at[i])
        for i, (src, dst) in enumerate(
            (
                (k_ref, k_buf),
                (v_ref, v_buf),
                (q_ref, q_buf),
                (counts_ref, counts_buf),
                (offsets_ref, offsets_buf),
                (w_ref.at[head], w_buf),
                (gain_ref, gain_buf),
            )
        )
    ]
    for load in loads:
        load.start()

    barrier = pltpu.get_barrier_semaphore()

    def greet(step, carry):
        pl.semaphore_signal(
            barrier, inc=1, device_id={"seq": partner(n - step)}, device_id_type=MESH
        )
        return carry

    lax.fori_loop(1, n, greet, 0)

    for load in loads[:3]:
        load.wait()

    for pair in range(heads // 2):
        lanes = slice(2 * width * pair, 2 * width * (pair + 1))
        k = k_buf[:, lanes]
        v = v_buf[:, lanes]
        kv_send[2 * pair] = jnp.concatenate([k[:, :width], v[:, :width]], axis=1)
        kv_send[2 * pair + 1] = jnp.concatenate([k[:, width:], v[:, width:]], axis=1)
        for piece in range(group):
            top = slice(piece * part_rows, piece * part_rows + part_half)
            low = slice(piece * part_rows + part_half, (piece + 1) * part_rows)
            a = q_buf[top, lanes]
            b = q_buf[low, lanes]
            q_send[2 * pair * group + piece] = jnp.concatenate([a[:, :width], b[:, :width]], axis=1)
            q_send[(2 * pair + 1) * group + piece] = jnp.concatenate(
                [a[:, width:], b[:, width:]], axis=1
            )

    pl.semaphore_wait(barrier, n - 1)

    def send_kv(step):
        peer = partner(step)
        return pltpu.make_async_remote_copy(
            src_ref=kv_send.at[peer // group],
            dst_ref=kv_recv.at[step],
            send_sem=kv_send_sem.at[step],
            recv_sem=kv_recv_sem.at[step],
            device_id={"seq": peer},
            device_id_type=MESH,
        )

    def send_q(step):
        peer = partner(step)
        return pltpu.make_async_remote_copy(
            src_ref=q_send.at[peer],
            dst_ref=q_recv.at[step],
            send_sem=q_send_sem.at[step],
            recv_sem=q_recv_sem.at[step],
            device_id={"seq": peer},
            device_id_type=MESH,
        )

    def back(step):
        return pltpu.make_async_remote_copy(
            src_ref=out_send.at[step],
            dst_ref=out_recv.at[step],
            send_sem=back_send_sem.at[step],
            recv_sem=back_recv_sem.at[step],
            device_id={"seq": partner(step)},
            device_id_type=MESH,
        )

    def start_near(step, carry):
        send_kv(step).start()
        send_q(step).start()
        return carry

    def start_kv(step, carry):
        send_kv(step).start()
        return carry

    def start_q(step, carry):
        send_q(step).start()
        return carry

    lax.fori_loop(1, near, start_near, 0)
    lax.fori_loop(near, n, start_kv, 0)
    lax.fori_loop(near, n, start_q, 0)
    kv_recv[0] = kv_send[head]
    q_recv[0] = q_send[me]

    for load in loads[3:]:
        load.wait()

    lane = lax.broadcasted_iota(jnp.int32, (n, rows), 1)
    start = jnp.zeros((n, 1), jnp.int32)
    position = lane
    for d in range(n):
        count = counts_buf[:, d : d + 1]
        inside = (lane >= start) & (lane < start + count)
        position = position + jnp.where(inside, d * rows + offsets_buf[:, d : d + 1] - start, 0)
        start = start + count
    position = position.astype(F32)
    posr[...] = position
    if n < rows:
        position = jnp.concatenate([position, jnp.zeros((rows - n, rows), F32)], axis=0)
    post[...] = position.T
    mine = post[pl.ds(pl.multiple_of(part * part_rows, part_rows), part_rows), :]
    for j in range(n):
        posc[j * part_rows : (j + 1) * part_rows, :] = jnp.broadcast_to(
            mine[:, j : j + 1], (part_rows, 128)
        )

    w = w_buf[...]
    blank = jnp.zeros_like(w)
    wqa[...] = jnp.concatenate([w, blank], axis=0)
    wqb[...] = jnp.concatenate([blank, w], axis=0)
    wkt[...] = wqa[...].astype(F32).T.astype(BF16)
    gain_row = gain_buf[...].astype(F32).reshape(1, -1)
    gain = jnp.zeros((1, width), F32)
    for h in range(heads):
        gain = gain + jnp.where(head == h, gain_row[:, h * width : (h + 1) * width], 0.0)

    def feature(z):
        return jnp.where(z > 0.0, z + 1.0, jnp.exp(jnp.minimum(z, 0.0))).astype(BF16)

    per = n // GROUPS
    tile_r = per * part_rows
    tile_s = per * rows

    def take_keys(g):
        x = kv_recv[g * per : (g + 1) * per].reshape(tile_s, 2 * width)
        keys = lax.dot_general(wkt[...], x, (((1,), (1,)), ((), ())), preferred_element_type=F32)
        phi_kt[:, g * tile_s : (g + 1) * tile_s] = feature(keys)

    def take_queries(first, count):
        x = q_recv[pl.ds(first, count)].reshape(count * part_half, 2 * width)
        top = jnp.dot(x, wqa[...], preferred_element_type=F32)
        low = jnp.dot(x, wqb[...], preferred_element_type=F32)
        return jnp.concatenate([feature(top), feature(low)], axis=0)

    def places(first, count):
        blocks = []
        for offset in (0, part_half):
            for i in range(count):
                at = partner(first + i) * part_rows + offset
                blocks.append(posc[pl.ds(pl.multiple_of(at, part_half), part_half), :])
        return jnp.concatenate(blocks, axis=0)

    def tile(phi, place, g):
        scores = jnp.dot(
            phi, phi_kt[:, g * tile_s : (g + 1) * tile_s], preferred_element_type=F32
        )
        later = jnp.concatenate([place] * per, axis=1)
        earlier = jnp.concatenate(
            [posr[pl.ds(partner(g * per + i), 1), :] for i in range(per)], axis=1
        )
        scores = jnp.where(earlier <= later, scores, 0.0)
        high = scores.astype(BF16)
        low = (scores - high.astype(F32)).astype(BF16)
        vals = kv_recv[g * per : (g + 1) * per].reshape(tile_s, 2 * width)
        return jnp.dot(high, vals, preferred_element_type=F32) + jnp.dot(
            low, vals, preferred_element_type=F32
        )

    def finish(first, count, attended):
        attended = attended[:, width:]
        centre = jnp.mean(attended, axis=1, keepdims=True)
        centred = attended - centre
        spread = jnp.mean(centred * centred, axis=1, keepdims=True)
        normed = (centred * lax.rsqrt(spread + 1e-05) * gain).astype(BF16)
        half = count * part_half
        packed = jnp.concatenate([normed[:half], normed[half:]], axis=1)
        out_send[pl.ds(first, count)] = packed.reshape(count, part_half, 2 * width)

    def rows_of(g):
        return slice(g * tile_r, (g + 1) * tile_r)

    nears = GROUPS // 2
    for g in range(GROUPS):
        for step in range(g * per, (g + 1) * per):
            if step > 0:
                send_kv(step).wait_recv()
                if g < nears:
                    send_q(step).wait_recv()
        take_keys(g)
        if g < nears:
            phi_q[rows_of(g), :] = take_queries(g * per, per)
            fresh = None
            for k in range(g + 1):
                more = tile(phi_q[rows_of(g), :], places(g * per, per), k)
                fresh = more if fresh is None else fresh + more
            acc[rows_of(g), :] = fresh
        for r in range(min(g, nears)):
            acc[rows_of(r), :] = acc[rows_of(r), :] + tile(
                phi_q[rows_of(r), :], places(r * per, per), g
            )
    for g in range(nears):
        finish(g * per, per, acc[rows_of(g), :])
        for step in range(g * per, (g + 1) * per):
            if step > 0:
                back(step).start()

    few = per // 2

    def late(piece, carry):
        first = near + piece * few
        for i in range(few):
            send_q(first + i).wait_recv()
        phi = take_queries(first, few)
        place = places(first, few)
        total = tile(phi, place, 0)
        for g in range(1, GROUPS):
            total = total + tile(phi, place, g)
        finish(first, few, total)
        for i in range(few):
            back(first + i).start()
        return carry

    lax.fori_loop(0, near // few, late, 0)
    out_recv[0] = out_send[0]

    def collect(step, carry):
        back(step).wait_recv()
        return carry

    lax.fori_loop(1, n, collect, 0)

    for piece in range(group):
        first = slice(piece * part_rows, piece * part_rows + part_half)
        second = slice(piece * part_rows + part_half, (piece + 1) * part_rows)
        for pair in range(heads // 2):
            lanes = slice(2 * width * pair, 2 * width * (pair + 1))
            a = out_recv[partner(2 * pair * group + piece)]
            b = out_recv[partner((2 * pair + 1) * group + piece)]
            out_ref[first, lanes] = jnp.concatenate([a[:, :width], b[:, :width]], axis=1)
            out_ref[second, lanes] = jnp.concatenate([a[:, width:], b[:, width:]], axis=1)

    def drain(step, carry):
        send_kv(step).wait_send()
        send_q(step).wait_send()
        back(step).wait_send()
        return carry

    lax.fori_loop(1, n, drain, 0)


def per_device(n, queries, keys, values, feat_weight, norm_gain, counts, offsets):
    rows = queries.shape[0]
    heads, width, feat = feat_weight.shape
    group = n // heads
    part_rows = rows // group
    total = n * rows
    lanes = 2 * width
    return pl.pallas_call(
        functools.partial(kernel, n, heads),
        out_shape=jax.ShapeDtypeStruct(queries.shape, BF16),
        in_specs=[pl.BlockSpec(memory_space=pltpu.HBM)] * 7,
        out_specs=pl.BlockSpec(memory_space=pltpu.VMEM),
        scratch_shapes=[
            pltpu.VMEM(queries.shape, BF16),
            pltpu.VMEM(keys.shape, BF16),
            pltpu.VMEM(values.shape, BF16),
            pltpu.VMEM((width, feat), BF16),
            pltpu.VMEM(norm_gain.shape, BF16),
            pltpu.VMEM(counts.shape, jnp.int32),
            pltpu.VMEM(offsets.shape, jnp.int32),
            pltpu.SemaphoreType.DMA((7,)),
            pltpu.VMEM((heads, rows, lanes), BF16),
            pltpu.VMEM((n, rows, lanes), BF16),
            pltpu.VMEM((n, part_rows // 2, lanes), BF16),
            pltpu.VMEM((n, part_rows // 2, lanes), BF16),
            pltpu.VMEM((feat, total), BF16),
            pltpu.VMEM((n * part_rows // 2, feat), BF16),
            pltpu.VMEM((n, rows), F32),
            pltpu.VMEM((rows, max(n, rows)), F32),
            pltpu.VMEM((n * part_rows, 128), F32),
            pltpu.VMEM((n * part_rows // 2, lanes), F32),
            pltpu.VMEM((lanes, feat), BF16),
            pltpu.VMEM((lanes, feat), BF16),
            pltpu.VMEM((feat, lanes), BF16),
            pltpu.VMEM((n, part_rows // 2, lanes), BF16),
            pltpu.VMEM((n, part_rows // 2, lanes), BF16),
            pltpu.SemaphoreType.DMA((n,)),
            pltpu.SemaphoreType.DMA((n,)),
            pltpu.SemaphoreType.DMA((n,)),
            pltpu.SemaphoreType.DMA((n,)),
            pltpu.SemaphoreType.DMA((n,)),
            pltpu.SemaphoreType.DMA((n,)),
        ],
        compiler_params=pltpu.CompilerParams(
            collective_id=0, has_side_effects=True, vmem_limit_bytes=67043328
        ),
    )(queries, keys, values, feat_weight, norm_gain, counts, offsets)


def solution(mesh):
    in_specs = (
        P(("dp", "seq"), None),
        P(("dp", "seq"), None),
        P(("dp", "seq"), None),
        P(),
        P(),
        P("dp", None),
        P("dp", None),
    )
    return jax.shard_map(
        functools.partial(per_device, mesh.shape["seq"]),
        mesh=mesh,
        in_specs=in_specs,
        out_specs=P(("dp", "seq"), None),
        check_vma=False,
    )
```

time: 39.6 us -> 38.8 us (0.980)
  local copies, waits for them, and re-layouts: 2.95 us -> 1.67 us
    reshape x1 -> x0, local copies, waits for them, and re-layouts: 1.28 us -> none  [per_device(): norm_gain.reshape(1, -1)]
where the time goes in v1:
time: 38.8 us; the launch traced here: 38.4 us
  Pallas kernels  36.7 us (95%)
  local copies, waits for them, and re-layouts  1.67 us (4%)
    pallas_call x1, Pallas kernels, per_device(): pl.pallas_call(functools.partial(kernel, n, heads), out_shape=jax.ShapeDt...  36.7 us
    unnamed x1, local copies, waits for them, and re-layouts  1.67 us

profile of v1, /device:TPU:0, one launch (start us, length us, event | category | flops | bytes accessed | tf_op | source)
XLA Modules:
  0.0 38.4 jit_solution(6237029258908029530)
XLA Ops:
  0.0 36.7 %shard_map.73 = bf16[128,1024]{1,0:T(8,128)(2,1)} custom-call(bf16[128,1024]{1,0:T(8,128)(2,1)} %q_ref.1, bf16[128,1024]{1,0:T(8,128)(2,1)} %k_ref.1, bf16[128,1024]{1,0:T(8,128)(2,1)} %v_ref.1, bf16[16,64,256]{2,1,0:T(8,128)(2,1)} %w_ref.1, bf16[1024]{0:T(1024)(128)(2,1)} %gain_ref.1, s32[16,16]{1,0:T(8,128)} %counts_ref.1, s32[16,16]{1,0:T(8,128)} %offsets_ref.1), custom_call_target="tpu_custom_call" | custom-call | tf_op jit(solution)/shard_map/pallas_call | solution.py:332
  36.7 1.7 %copy.9 = bf16[128,1024]{1,0:T(8,128)(2,1)} copy(bf16[128,1024]{1,0:T(8,128)(2,1)} %shard_map.73) | data formatting | bytes 524288
